TPU v7x, 512 devices: a whole 4x8x8 slice. The times are simulated.
512 devices in a mesh: dp: 16 (over y_lo, x), tile: 32 (over y_hi, z, core).
Axes of the slice: x: 4, y: 8 (y_hi: 2, y_lo: 4; y = y_hi * 4 + y_lo), z: 8, core: 2. Of those that a mesh axis runs over, the one named last changes fastest.
Arguments:
- features: bfloat16 [16, 32, 8, 16, 1024], P('dp', 'tile'), may hold values from -6 to 6
- cotangent: bfloat16 [16, 32, 8, 16, 1024], P('dp', 'tile'), may hold values from -6 to 6
- in_weight: bfloat16 [3072, 1024], P(('dp', 'tile')), may hold values from -0.1875 to 0.1875
- out_weight: bfloat16 [3072, 1024], P(('dp', 'tile')), may hold values from -0.109375 to 0.109375
- hidden_bias: bfloat16 [3072], P(('dp', 'tile')), may hold values from -3 to 3
- kernel: float32 [49, 1024], P(None, 'dp'), may hold values from -0.875 to 0.875
- conv_bias: float32 [1024], P('dp'), may hold values from -3 to 3
- norm_gain: float32 [1024], P('dp'), may hold values from 0.5 to 1.5
- norm_bias: float32 [1024], P('dp'), may hold values from -3 to 3
- layer_scale: float32 [1024], P('dp'), may hold values from 0.5 to 1.5
- out_bias: float32 [1024], P('dp'), may hold values from -3 to 3
Outputs:
- block_out: bfloat16 [16, 32, 8, 16, 1024], P('dp', 'tile')
- grad_input: bfloat16 [16, 32, 8, 16, 1024], P('dp', 'tile')
- grad_kernel: float32 [49, 1024], P(None, 'dp')
- grad_conv_bias: float32 [1024], P('dp')
- grad_norm_gain: float32 [1024], P('dp')
- grad_norm_bias: float32 [1024], P('dp')
- grad_layer_scale: float32 [1024], P('dp')
All inputs are finite; a program needn't handle non-finite values.
Results may differ from a plain program's by a relative error of at most 0.0061.
Values may be sent and summed in bfloat16 or wider, within the bound.
A program may use at most 128 MiB of HBM per device.

v0:
```python
import math
import jax
import jax.numpy as jnp
from jax import lax
from jax.sharding import PartitionSpec as P

KS = 7
GX = 4


def passed_along(block, axis, distance):
    devices = range(lax.axis_size(axis))
    route = [(i - distance, i) for i in devices if i - distance in devices]
    return lax.ppermute(block, axis, route)


def gelu_exact(values):
    return 0.5 * values * (1.0 + jax.scipy.special.erf(values * 0.7071067811865476))


def gelu_slope(values):
    return (
        0.5 * (1.0 + jax.scipy.special.erf(values * 0.7071067811865476))
        + values * jnp.exp(-0.5 * values * values) * 0.3989422804014327
    )


def edge_part(field, step, axis):
    length = field.shape[axis]
    margin = KS // 2
    if step < 0:
        return lax.slice_in_dim(field, length - margin, length, axis=axis)
    if step > 0:
        return lax.slice_in_dim(field, 0, margin, axis=axis)
    return field


def pad_field(field, row_place, col_place, grid_rows):
    bands = []
    for row_step in (-1, 0, 1):
        pieces = []
        for col_step in (-1, 0, 1):
            if row_step == 0 and col_step == 0:
                pieces.append(field)
            else:
                border = edge_part(edge_part(field, row_step, 1), col_step, 2)
                moved = passed_along(border, "tile", -(row_step * GX + col_step))
                row_new = row_place + row_step
                col_new = col_place + col_step
                pieces.append(
                    jnp.where(
                        (row_new >= 0) & (row_new < grid_rows) & (col_new >= 0) & (col_new < GX),
                        moved,
                        jnp.zeros_like(moved),
                    )
                )
        bands.append(jnp.concatenate(pieces, axis=2))
    return jnp.concatenate(bands, axis=1)


def per_device(
    features,
    cotangent,
    in_weight,
    out_weight,
    hidden_bias,
    kernel,
    conv_bias,
    norm_gain,
    norm_bias,
    layer_scale,
    out_bias,
):
    image_count, _, rows, cols, width = features.shape
    tile_count = lax.axis_size("tile")
    grid_rows = tile_count // GX
    place = lax.axis_index("tile")
    row_place = place // GX
    col_place = place % GX
    margin = KS // 2
    kernel_all, cbias, gain, nbias, lscale, obias = (
        lax.all_gather(kernel, "dp", axis=1, tiled=True),
        lax.all_gather(conv_bias, "dp", axis=0, tiled=True),
        lax.all_gather(norm_gain, "dp", axis=0, tiled=True),
        lax.all_gather(norm_bias, "dp", axis=0, tiled=True),
        lax.all_gather(layer_scale, "dp", axis=0, tiled=True),
        lax.all_gather(out_bias, "dp", axis=0, tiled=True),
    )
    picture = features.reshape(image_count, rows, cols, width)
    padded = pad_field(picture, row_place, col_place, grid_rows)
    convolved = jnp.zeros((image_count, rows, cols, width), jnp.float32) + cbias
    for tap_row in range(KS):
        for tap_col in range(KS):
            window = padded[:, tap_row : tap_row + rows, tap_col : tap_col + cols, :].astype(
                jnp.float32
            )
            convolved = convolved + kernel_all[tap_row * KS + tap_col] * window
    average = jnp.mean(convolved, axis=-1, keepdims=True)
    centered = convolved - average
    variance = jnp.mean(centered * centered, axis=-1, keepdims=True)
    inverse = lax.rsqrt(variance + 1e-06)
    pixel_rows = image_count * rows * cols
    standard = (centered * inverse).reshape(pixel_rows, width)
    inverse = inverse.reshape(pixel_rows, 1)
    normed = (standard * gain + nbias).astype(jnp.bfloat16)
    upstream = cotangent.reshape(pixel_rows, width).astype(jnp.float32)
    back_out = (upstream * lscale).astype(jnp.bfloat16)
    rows_in = lax.all_gather(in_weight, ("dp", "tile"), axis=0, tiled=True)
    rows_out = lax.all_gather(out_weight, ("dp", "tile"), axis=0, tiled=True)
    bias_part = lax.all_gather(hidden_bias, ("dp", "tile"), axis=0, tiled=True)
    pre = lax.dot_general(
        normed, rows_in, (((1,), (1,)), ((), ())), preferred_element_type=jnp.float32
    ) + bias_part.astype(jnp.float32)
    hidden = gelu_exact(pre).astype(jnp.bfloat16)
    mlp_sum = jnp.dot(hidden, rows_out, preferred_element_type=jnp.float32)
    back_hidden = lax.dot_general(
        back_out, rows_out, (((1,), (1,)), ((), ())), preferred_element_type=jnp.float32
    )
    back_pre = (back_hidden * gelu_slope(pre)).astype(jnp.bfloat16)
    normed_sum = jnp.dot(back_pre, rows_in, preferred_element_type=jnp.float32)
    mlp_sum, back_normed = (mlp_sum, normed_sum)
    projected = mlp_sum + obias
    source = picture.reshape(pixel_rows, width).astype(jnp.float32)
    block_out = (source + lscale * projected).astype(jnp.bfloat16).reshape(features.shape)
    scale_part = jnp.sum(upstream * projected, axis=0)
    gain_part = jnp.sum(back_normed * standard, axis=0)
    nbias_part = jnp.sum(back_normed, axis=0)
    scaled = back_normed * gain
    back_conv = inverse * (
        scaled
        - jnp.mean(scaled, axis=-1, keepdims=True)
        - standard * jnp.mean(scaled * standard, axis=-1, keepdims=True)
    )
    cbias_part = jnp.sum(back_conv, axis=0)
    back_grid = back_conv.reshape(image_count, rows, cols, width)
    back_padded = pad_field(back_grid.astype(jnp.bfloat16), row_place, col_place, grid_rows)
    grad_grid = upstream.reshape(image_count, rows, cols, width)
    kernel_rows = []
    for tap_row in range(KS):
        for tap_col in range(KS):
            tap_weight = kernel_all[tap_row * KS + tap_col]
            flipped = back_padded[
                :,
                2 * margin - tap_row : 2 * margin - tap_row + rows,
                2 * margin - tap_col : 2 * margin - tap_col + cols,
                :,
            ].astype(jnp.float32)
            grad_grid = grad_grid + tap_weight * flipped
            window = padded[:, tap_row : tap_row + rows, tap_col : tap_col + cols, :].astype(
                jnp.float32
            )
            kernel_rows.append(jnp.sum(back_grid * window, axis=(0, 1, 2)))
    grad_input = grad_grid.astype(jnp.bfloat16).reshape(features.shape)
    kernel_terms = jnp.stack(kernel_rows)
    shared = (
        lax.psum_scatter(kernel_terms, "dp", scatter_dimension=1, tiled=True),
        lax.psum_scatter(cbias_part, "dp", scatter_dimension=0, tiled=True),
        lax.psum_scatter(gain_part, "dp", scatter_dimension=0, tiled=True),
        lax.psum_scatter(nbias_part, "dp", scatter_dimension=0, tiled=True),
        lax.psum_scatter(scale_part, "dp", scatter_dimension=0, tiled=True),
    )
    kernel_sum, cbias_sum, gain_sum, nbias_sum, scale_sum = lax.psum(
        (shared[0], shared[1], shared[2], shared[3], shared[4]), "tile"
    )
    factor = 1.0 / math.sqrt(image_count * lax.axis_size("dp") * rows * cols * tile_count)
    return (
        block_out,
        grad_input,
        kernel_sum * factor,
        cbias_sum * factor,
        gain_sum * factor,
        nbias_sum * factor,
        scale_sum * factor,
    )


def solution(mesh):
    placed = (
        P("dp", "tile", None, None, None),
        P("dp", "tile", None, None, None),
        P(("dp", "tile"), None),
        P(("dp", "tile"), None),
        P(("dp", "tile")),
        P(None, "dp"),
        P("dp"),
        P("dp"),
        P("dp"),
        P("dp"),
        P("dp"),
    )
    return jax.shard_map(
        per_device,
        mesh=mesh,
        in_specs=placed,
        out_specs=(
            P("dp", "tile", None, None, None),
            P("dp", "tile", None, None, None),
            P(None, "dp"),
            P("dp"),
            P("dp"),
            P("dp"),
            P("dp"),
        ),
        check_vma=False,
    )
```

profile of v0, /device:TPU:62, one launch (start us, length us, event | category | flops | bytes accessed | tf_op | source)
XLA Modules:
  0.0 2041.7 jit_solution(7205430439878918634)
XLA Ops:
  9.6 5.5 collective-permute-start
  15.2 9.0 collective-permute-start.7
  24.2 4.6 collective-permute-start.5
  35.4 39.3 %all-gather = f32[16,64,49]{1,2,0:T(8,128)S(1)} all-gather(f32[1,64,49]{1,2,0:T(8,128)} %bitcast.363), channel_id=1, replica_groups=mesh['dp'=16,'tile'=32] {'dp'}, dimensions={0}, use_global_device_ids=true | all-gather | bytes 213248 | tf_op jit(solution)/shard_map/all_gather | solution.py:82
  76.5 99.9 %all-reduce.4 = bf16[3072]{0:T(1024)(128)(2,1)S(1)} all-reduce(bf16[3072]{0:T(1024)(128)(2,1)S(1)} %dynamic-update-slice.4), channel_id=1, replica_groups=mesh['dp'=16,'tile'=32] {'dp','tile'}, use_global_device_ids=true, to_apply=%add.4 | all-reduce | flops 3072 | bytes 12288
  179.5 73.9 %all-reduce.12 = (f32[1024]{0:T(1024)S(1)}, f32[1024]{0:T(1024)S(1)}, f32[1024]{0:T(1024)}, f32[1024]{0:T(1024)}, f32[1024]{0:T(1024)}) all-reduce(f32[1024]{0:T(1024)S(1)} %dynamic-update-slice.1, f32[1024]{0:T(1024)S(1)} %dynamic-update-slice.3, f32[1024]{0:T(1024)S(1)} %dynamic-update-slice.2, ...), channel_id=1, replica_groups=mesh['dp'=16,'tile'=32] {'dp'}, use_global_device_ids=true, to_apply=%add.1 | all-reduce | flops 5120 | bytes 40960
  257.5 10.6 collective-permute-start.6
  272.1 6.5 fusion.155
  281.1 552.5 %all-gather.6.cloned.1.call-done = bf16[512,6,1024]{2,1,0:T(8,128)(2,1)} async-done(((bf16[1,6,1024]{2,1,0:T(8,128)(2,1)}), bf16[512,6,1024]{2,1,0:T(8,128)(2,1)}) %all-gather.6.cloned.1.call-update) | async-done | bytes 6291472 | tf_op jit(solution)/shard_map/all_gather | solution.py:108
  833.6 11.0 reshape.319
  844.6 5.1 convolution_add_fusion
  849.8 803.6 %all-gather.8.cloned.1.call-done = bf16[512,6,1024]{2,1,0:T(8,128)(2,1)} async-done(((bf16[1,6,1024]{2,1,0:T(8,128)(2,1)}), bf16[512,6,1024]{2,1,0:T(8,128)(2,1)}) %all-gather.8.cloned.1.call-update) | async-done | bytes 6291472 | tf_op jit(solution)/shard_map/all_gather | solution.py:109
  1653.4 11.1 reshape.321
  1664.5 5.3 fusion.133
  1669.7 9.4 fusion.139
  1687.7 73.8 %all-reduce.11 = (f32[1024]{0:T(1024)S(1)}, f32[1024]{0:T(1024)S(1)}, f32[1024]{0:T(1024)S(1)}, f32[1024]{0:T(1024)S(1)}) all-reduce(f32[1024]{0:T(1024)S(1)} %get-tuple-element.62, f32[1024]{0:T(1024)S(1)} %copy-done.83, f32[1024]{0:T(1024)S(1)} %copy-done.84, f32[1024]{0:T(1024)S(1)} %copy-done.80), channel_id=3, replica_groups=mesh['dp'=16,'tile'=32] {'dp'}, use_global_device_ids=true, to_apply=%region_56.57.clone | all-reduce | flops 4096 | bytes 32768
  1763.8 6.5 collective-permute-start.15
  1770.3 6.9 collective-permute-start.12
  1781.0 9.6 collective-permute-start.9
  1792.6 4.8 collective-permute-start.14
  1798.0 8.3 collective-permute-done.14
  1807.0 5.7 fusion.148
  1812.8 51.9 %reduce-scatter.4.cloned.1.call-done = f32[64,49]{1,0:T(8,128)} async-done(((f32[1024,49]{1,0:T(8,128)}), f32[64,49]{1,0:T(8,128)}) %reduce-scatter.4.cloned.1.call-update) | async-done | bytes 12560
  1865.5 167.0 %all-reduce.10 = (f32[49,64]{1,0:T(8,128)S(1)}, f32[64]{0:T(128)S(1)}, f32[64]{0:T(128)S(1)}, f32[64]{0:T(128)S(1)}, f32[64]{0:T(128)S(1)}) all-reduce(f32[49,64]{1,0:T(8,128)S(1)} %copy.21, f32[64]{0:T(128)S(1)} %dynamic-slice.6, f32[64]{0:T(128)S(1)} %dynamic-slice.8, ...), channel_id=1, replica_groups=mesh['dp'=16,'tile'=32] {'tile'}, use_global_device_ids=true, to_apply=%region_54.55 | all-reduce | flops 3392 | bytes 27136 | tf_op jit(solution)/shard_map/psum | solution.py:162
  (280 shorter events, 42.9 us)
Async XLA Ops:
  7.2 826.4 %all-gather.6.cloned.1.call-start = ((), (), s32[]{:S(2)}) async-start(), calls=%async_computation.1 | async-start | bytes 8404992 | tf_op jit(solution)/shard_map/all_gather | solution.py:108
  7.9 1645.5 %all-gather.8.cloned.1.call-start = ((), (), s32[]{:S(2)}) async-start(), calls=%async_computation.2 | async-start | bytes 8404992 | tf_op jit(solution)/shard_map/all_gather | solution.py:109
  8.7 1856.0 %reduce-scatter.4.cloned.1.call-start = ((), (), s32[]{:S(2)}) async-start(), calls=%async_computation.3 | async-start | bytes 557056
  9.6 243.7 %collective-permute-start = (bf16[1,3,3,1024]{3,2,1,0:T(4,128)(2,1)S(1)}, bf16[1,3,3,1024]{3,2,1,0:T(4,128)(2,1)S(1)}, u32[]{:S(2)}, u32[]{:S(2)}) collective-permute-start(bf16[1,3,3,1024]{3,2,1,0:T(4,128)(2,1)S(1)} %get-tuple-element.105), channel_id=1, source_target_pairs={{0,5},{1,6},{2,7},{3,8},{4,9},{5,10},{6,11},{7,12},{8,13},{9,14},{... | collective-permute-start | bytes 55304 | tf_op jit(solution)/shard_map/ppermute | solution.py:14
  15.2 240.1 %collective-permute-start.7 = (bf16[1,3,3,1024]{3,2,1,0:T(4,128)(2,1)S(1)}, bf16[1,3,3,1024]{3,2,1,0:T(4,128)(2,1)S(1)}, u32[]{:S(2)}, u32[]{:S(2)}) collective-permute-start(bf16[1,3,3,1024]{3,2,1,0:T(4,128)(2,1)S(1)} %get-tuple-element.106), channel_id=1, source_target_pairs={{5,0},{6,1},{7,2},{8,3},{9,4},{10,5},{11,6},{12,7},{13,8},{14,9},{... | collective-permute-start | bytes 55304 | tf_op jit(solution)/shard_map/ppermute | solution.py:14
  24.2 233.3 %collective-permute-start.5 = (bf16[1,3,3,1024]{3,2,1,0:T(4,128)(2,1)S(1)}, bf16[1,3,3,1024]{3,2,1,0:T(4,128)(2,1)S(1)}, u32[]{:S(2)}, u32[]{:S(2)}) collective-permute-start(bf16[1,3,3,1024]{3,2,1,0:T(4,128)(2,1)S(1)} %get-tuple-element.107), channel_id=1, source_target_pairs={{3,0},{4,1},{5,2},{6,3},{7,4},{8,5},{9,6},{10,7},{11,8},{12,9},{13... | collective-permute-start | bytes 55304 | tf_op jit(solution)/shard_map/ppermute | solution.py:14
  28.8 239.3 %collective-permute-start.2 = (bf16[1,3,3,1024]{3,2,1,0:T(4,128)(2,1)S(1)}, bf16[1,3,3,1024]{3,2,1,0:T(4,128)(2,1)S(1)}, u32[]{:S(2)}, u32[]{:S(2)}) collective-permute-start(bf16[1,3,3,1024]{3,2,1,0:T(4,128)(2,1)S(1)} %get-tuple-element.108), channel_id=1, source_target_pairs={{0,3},{1,4},{2,5},{3,6},{4,7},{5,8},{6,9},{7,10},{8,11},{9,12},{10... | collective-permute-start | bytes 55304 | tf_op jit(solution)/shard_map/ppermute | solution.py:14
  31.9 236.3 %collective-permute-start.3 = (bf16[1,8,3,1024]{3,2,1,0:T(4,128)(2,1)S(1)}, bf16[1,8,3,1024]{3,2,1,0:T(4,128)(2,1)S(1)}, u32[]{:S(2)}, u32[]{:S(2)}) collective-permute-start(bf16[1,8,3,1024]{3,2,1,0:T(4,128)(2,1)S(1)} %get-tuple-element.111), channel_id=1, source_target_pairs={{0,1},{1,2},{2,3},{3,4},{4,5},{5,6},{6,7},{7,8},{8,9},{9,10},{10,1... | collective-permute-start | bytes 147464 | tf_op jit(solution)/shard_map/ppermute | solution.py:14
  76.1 202.6 %copy-start.70 = (f32[1,1024]{1,0:T(1,128)}, f32[1,1024]{1,0:T(1,128)S(1)}, u32[]{:S(2)}) copy-start(f32[1,1024]{1,0:T(1,128)S(1)} %get-tuple-element.155) | copy-start | bytes 12292
  76.1 202.6 %copy-start.72 = (f32[1,1024]{1,0:T(1,128)}, f32[1,1024]{1,0:T(1,128)S(1)}, u32[]{:S(2)}) copy-start(f32[1,1024]{1,0:T(1,128)S(1)} %get-tuple-element.156) | copy-start | bytes 12292
  76.1 202.6 %copy-start.74 = (f32[1,1024]{1,0:T(1,128)}, f32[1,1024]{1,0:T(1,128)S(1)}, u32[]{:S(2)}) copy-start(f32[1,1024]{1,0:T(1,128)S(1)} %get-tuple-element.157) | copy-start | bytes 12292
  253.4 14.9 collective-permute-start.4
  255.3 16.1 collective-permute-start.1
  257.5 14.0 collective-permute-start.6
  849.7 814.7 %copy-start.81 = (f32[1024]{0:T(1024)S(1)}, f32[1024]{0:T(1024)}, u32[]{:S(2)}) copy-start(f32[1024]{0:T(1024)} %get-tuple-element.85) | copy-start | bytes 12292
  849.8 814.7 %copy-start.82 = (f32[1024]{0:T(1024)S(1)}, f32[1024]{0:T(1024)}, u32[]{:S(2)}) copy-start(f32[1024]{0:T(1024)} %get-tuple-element.86) | copy-start | bytes 12292
  1683.9 97.1 %collective-permute-start.10 = (bf16[1,3,3,1024]{3,2,1,0:T(4,128)(2,1)S(1)}, bf16[1,3,3,1024]{3,2,1,0:T(4,128)(2,1)S(1)}, u32[]{:S(2)}, u32[]{:S(2)}) collective-permute-start(bf16[1,3,3,1024]{3,2,1,0:T(4,128)(2,1)S(1)} %get-tuple-element.97), channel_id=1, source_target_pairs={{3,0},{4,1},{5,2},{6,3},{7,4},{8,5},{9,6},{10,7},{11,8},{12,9},{13... | collective-permute-start | bytes 55304 | tf_op jit(solution)/shard_map/ppermute | solution.py:14
  1761.9 28.7 %collective-permute-start.13 = (bf16[1,3,3,1024]{3,2,1,0:T(4,128)(2,1)S(1)}, bf16[1,3,3,1024]{3,2,1,0:T(4,128)(2,1)S(1)}, u32[]{:S(2)}, u32[]{:S(2)}) collective-permute-start(bf16[1,3,3,1024]{3,2,1,0:T(4,128)(2,1)S(1)} %get-tuple-element.98), channel_id=1, source_target_pairs={{0,5},{1,6},{2,7},{3,8},{4,9},{5,10},{6,11},{7,12},{8,13},{9,14},{... | collective-permute-start | bytes 55304 | tf_op jit(solution)/shard_map/ppermute | solution.py:14
  1763.8 28.8 %collective-permute-start.15 = (bf16[1,3,3,1024]{3,2,1,0:T(4,128)(2,1)S(1)}, bf16[1,3,3,1024]{3,2,1,0:T(4,128)(2,1)S(1)}, u32[]{:S(2)}, u32[]{:S(2)}) collective-permute-start(bf16[1,3,3,1024]{3,2,1,0:T(4,128)(2,1)S(1)} %get-tuple-element.99), channel_id=1, source_target_pairs={{0,3},{1,4},{2,5},{3,6},{4,7},{5,8},{6,9},{7,10},{8,11},{9,12},{10... | collective-permute-start | bytes 55304 | tf_op jit(solution)/shard_map/ppermute | solution.py:14
  1770.3 27.2 %collective-permute-start.12 = (bf16[1,3,3,1024]{3,2,1,0:T(4,128)(2,1)S(1)}, bf16[1,3,3,1024]{3,2,1,0:T(4,128)(2,1)S(1)}, u32[]{:S(2)}, u32[]{:S(2)}) collective-permute-start(bf16[1,3,3,1024]{3,2,1,0:T(4,128)(2,1)S(1)} %get-tuple-element.100), channel_id=1, source_target_pairs={{5,0},{6,1},{7,2},{8,3},{9,4},{10,5},{11,6},{12,7},{13,8},{14,9},{... | collective-permute-start | bytes 55304 | tf_op jit(solution)/shard_map/ppermute | solution.py:14
  1777.2 20.3 collective-permute-start.8
  1781.0 16.5 collective-permute-start.9
  1790.6 7.4 collective-permute-start.11
  1792.6 13.7 collective-permute-start.14
  (87 other events, 8975.9 us)
Sparse Core Ops, SparseCore 0:
  10.2 823.3 all-gather.5
  835.8 817.5 all-gather.7
  1781.1 83.4 reduce-scatter.3
where the time goes:
time: 2040 us
  waiting for transfers between devices  1420 us (70%)
  blocking collectives  454 us (22%)
  starting transfers between devices  76.7 us (4%)
  local copies, waits for them, and re-layouts  30.7 us (2%)
  other arithmetic  22.4 us (1%)
    all_gather x1, waiting for transfers between devices, per_device(): rows_out = lax.all_gather(out_weight, ('dp', 'tile'), axis=0, tiled=True)  804 us
    all_gather x1, waiting for transfers between devices, per_device(): rows_in = lax.all_gather(in_weight, ('dp', 'tile'), axis=0, tiled=True)  552 us
    unnamed x3, blocking collectives  248 us
    psum x1, blocking collectives, per_device(): lax.psum((shared[0], shared[1], shared[2], shared[3], shared[4]), 'tile')  167 us
    ppermute x16, starting transfers between devices, passed_along(): return lax.ppermute(block, axis, route)  76.6 us
    unnamed x4, waiting for transfers between devices  53.3 us
  transfers between devices with their start and end apart: 19, of which 6 were waited for; matrix products, arithmetic and copies ran while one was open for 2% of the time, Pallas kernels for 0%

commit v1 on v0

--- a/solution.py
+++ b/solution.py
@@ -106,7 +106,12 @@
     upstream = cotangent.reshape(pixel_rows, width).astype(jnp.float32)
     back_out = (upstream * lscale).astype(jnp.bfloat16)
     rows_in = lax.all_gather(in_weight, ("dp", "tile"), axis=0, tiled=True)
-    rows_out = lax.all_gather(out_weight, ("dp", "tile"), axis=0, tiled=True)
+    rows_out = jnp.concatenate(
+        lax.all_to_all(
+            jnp.stack([out_weight] * lax.axis_size(("dp", "tile"))), ("dp", "tile"), 0, 0
+        ),
+        axis=0,
+    )
     bias_part = lax.all_gather(hidden_bias, ("dp", "tile"), axis=0, tiled=True)
     pre = lax.dot_general(
         normed, rows_in, (((1,), (1,)), ((), ())), preferred_element_type=jnp.float32

time: 2040 us -> 1360 us (0.67)
  the two profiles are of different devices: /device:TPU:62 before, /device:TPU:32 now
where the time goes in v1:
time: 1360 us
  blocking collectives  629 us (46%)
  waiting for transfers between devices  553 us (41%)
  starting transfers between devices  84.8 us (6%)
  local copies, waits for them, and re-layouts  36 us (3%)
  other arithmetic  25 us (2%)
  between operations  17.8 us (1%)
  matrix products  16.5 us (1%)
    all_gather x1, waiting for transfers between devices, per_device(): rows_in = lax.all_gather(in_weight, ('dp', 'tile'), axis=0, tiled=True)  534 us
    unnamed x3, blocking collectives  263 us
    all_gather x1, blocking collectives, per_device(): lax.all_gather(kernel, 'dp', axis=1, tiled=True)  199 us
    psum x1, blocking collectives, per_device(): lax.psum((shared[0], shared[1], shared[2], shared[3], shared[4]), 'tile')  167 us
    ppermute x16, starting transfers between devices, passed_along(): return lax.ppermute(block, axis, route)  61.7 us
  transfers between devices with their start and end apart: 19, of which 4 were waited for; matrix products, arithmetic and copies ran while one was open for 3% of the time, Pallas kernels for 0%

profile of v1, /device:TPU:32, one launch (start us, length us, event | category | flops | bytes accessed | tf_op | source)
XLA Modules:
  0.0 1361.6 jit_solution(13693805816076579156)
XLA Ops:
  7.9 5.0 stack.102
  12.9 23.0 %all-to-all-start = ((bf16[512,6,1024]{2,1,0:T(8,128)(2,1)}), bf16[512,6,1024]{2,1,0:T(8,128)(2,1)}, u32[]{:S(2)}, u32[]{:S(2)}) async-start(bf16[512,6,1024]{2,1,0:T(8,128)(2,1)} %stack.102), calls=%async_computation | async-start | bytes 16777216 | tf_op jit(solution)/shard_map/all_to_all | solution.py:110
  36.1 7.8 collective-permute-start.4
  47.9 4.3 collective-permute-start.1
  55.6 198.8 %all-gather = f32[16,64,49]{1,2,0:T(8,128)S(1)} all-gather(f32[1,64,49]{1,2,0:T(8,128)S(1)} %bitcast.361), channel_id=1, replica_groups=mesh['dp'=16,'tile'=32] {'dp'}, dimensions={0}, use_global_device_ids=true | all-gather | bytes 213248 | tf_op jit(solution)/shard_map/all_gather | solution.py:82
  257.2 76.4 %all-reduce.12 = (f32[1024]{0:T(1024)S(1)}, f32[1024]{0:T(1024)S(1)}, f32[1024]{0:T(1024)}, f32[1024]{0:T(1024)}, f32[1024]{0:T(1024)S(1)}) all-reduce(f32[1024]{0:T(1024)S(1)} %dynamic-update-slice.1, f32[1024]{0:T(1024)S(1)} %dynamic-update-slice.3, f32[1024]{0:T(1024)S(1)} %dynamic-update-slice.2, ...), channel_id=1, replica_groups=mesh['dp'=16,'tile'=32] {'dp'}, use_global_device_ids=true, to_apply=%add.1 | all-reduce | flops 5120 | bytes 40960
  335.8 101.6 %all-reduce.4 = bf16[3072]{0:T(1024)(128)(2,1)S(1)} all-reduce(bf16[3072]{0:T(1024)(128)(2,1)S(1)} %dynamic-update-slice.4), channel_id=1, replica_groups=mesh['dp'=16,'tile'=32] {'dp','tile'}, use_global_device_ids=true, to_apply=%add.4 | all-reduce | flops 3072 | bytes 12288
  438.0 4.9 collective-permute-start.7
  443.0 3.8 collective-permute-start.6
  446.8 7.8 collective-permute-start.5
  456.8 6.5 fusion.153
  465.8 534.1 %all-gather.4.cloned.1.call-done = bf16[512,6,1024]{2,1,0:T(8,128)(2,1)} async-done(((bf16[1,6,1024]{2,1,0:T(8,128)(2,1)}), bf16[512,6,1024]{2,1,0:T(8,128)(2,1)}) %all-gather.4.cloned.1.call-update) | async-done | bytes 6291472 | tf_op jit(solution)/shard_map/all_gather | solution.py:108
  999.8 11.1 reshape.330
  1010.9 5.1 convolution_add_fusion
  1016.0 11.1 reshape.303
  1027.1 9.3 fusion.137
  1048.2 7.3 collective-permute-start.11
  1055.5 4.2 collective-permute-start.10
  1067.5 84.7 %all-reduce.11 = (f32[1024]{0:T(1024)S(1)}, f32[1024]{0:T(1024)S(1)}, f32[1024]{0:T(1024)S(1)}, f32[1024]{0:T(1024)S(1)}) all-reduce(f32[1024]{0:T(1024)S(1)} %get-tuple-element.97, f32[1024]{0:T(1024)} %get-tuple-element.49, f32[1024]{0:T(1024)} %get-tuple-element.61, ...), channel_id=3, replica_groups=mesh['dp'=16,'tile'=32] {'dp'}, use_global_device_ids=true, to_apply=%region_56.57.clone | all-reduce | flops 4096 | bytes 32768
  1154.5 4.2 collective-permute-start.14
  1158.7 5.9 collective-permute-done.15
  1166.5 11.0 collective-permute-done.13
  1178.5 5.8 fusion.146
  1185.1 167.0 %all-reduce.10 = (f32[49,64]{1,0:T(8,128)S(1)}, f32[64]{0:T(128)S(1)}, f32[64]{0:T(128)S(1)}, f32[64]{0:T(128)S(1)}, f32[64]{0:T(128)S(1)}) all-reduce(f32[49,64]{1,0:T(8,128)S(1)} %copy.21, f32[64]{0:T(128)S(1)} %dynamic-slice.6, f32[64]{0:T(128)S(1)} %dynamic-slice.8, ...), channel_id=1, replica_groups=mesh['dp'=16,'tile'=32] {'tile'}, use_global_device_ids=true, to_apply=%region_54.55 | all-reduce | flops 3392 | bytes 27136 | tf_op jit(solution)/shard_map/psum | solution.py:167
  (353 shorter events, 43.2 us)
Async XLA Ops:
  7.2 992.7 %all-gather.4.cloned.1.call-start = ((), (), s32[]{:S(2)}) async-start(), calls=%async_computation.2 | async-start | bytes 8404992 | tf_op jit(solution)/shard_map/all_gather | solution.py:108
  12.9 1003.1 %all-to-all-start = ((bf16[512,6,1024]{2,1,0:T(8,128)(2,1)}), bf16[512,6,1024]{2,1,0:T(8,128)(2,1)}, u32[]{:S(2)}, u32[]{:S(2)}) async-start(bf16[512,6,1024]{2,1,0:T(8,128)(2,1)} %stack.102), calls=%async_computation | async-start | bytes 16777216 | tf_op jit(solution)/shard_map/all_to_all | solution.py:110
  35.9 220.6 %copy-start.122 = (f32[64]{0:T(128)S(1)}, f32[64]{0:T(128)}, u32[]{:S(2)}) copy-start(f32[64]{0:T(128)} %param.18) | copy-start | bytes 772
  35.9 220.8 %copy-start.123 = (f32[64]{0:T(128)S(1)}, f32[64]{0:T(128)}, u32[]{:S(2)}) copy-start(f32[64]{0:T(128)} %param.21) | copy-start | bytes 772
  35.9 221.0 %copy-start.124 = (f32[64]{0:T(128)S(1)}, f32[64]{0:T(128)}, u32[]{:S(2)}) copy-start(f32[64]{0:T(128)} %param.20) | copy-start | bytes 772
  36.0 1148.3 %reduce-scatter.4.cloned.1.call-start = ((), (), s32[]{:S(2)}) async-start(), calls=%async_computation.3 | async-start | bytes 557056
  36.0 298.0 %copy-start.1 = (bf16[1,1,8,16,1024]{4,3,2,1,0:T(8,128)(2,1)S(1)}, bf16[1,1,8,16,1024]{4,3,2,1,0:T(8,128)(2,1)}, u32[]{:S(2)}) copy-start(bf16[1,1,8,16,1024]{4,3,2,1,0:T(8,128)(2,1)} %param.12) | copy-start | bytes 786436
  36.1 419.9 %collective-permute-start.4 = (bf16[1,8,3,1024]{3,2,1,0:T(4,128)(2,1)S(1)}, bf16[1,8,3,1024]{3,2,1,0:T(4,128)(2,1)S(1)}, u32[]{:S(2)}, u32[]{:S(2)}) collective-permute-start(bf16[1,8,3,1024]{3,2,1,0:T(4,128)(2,1)S(1)} %get-tuple-element.113), channel_id=1, source_target_pairs={{1,0},{2,1},{3,2},{4,3},{5,4},{6,5},{7,6},{8,7},{9,8},{10,9},{11,1... | collective-permute-start | bytes 147464 | tf_op jit(solution)/shard_map/ppermute | solution.py:14
  43.9 412.1 %collective-permute-start.3 = (bf16[1,8,3,1024]{3,2,1,0:T(4,128)(2,1)S(1)}, bf16[1,8,3,1024]{3,2,1,0:T(4,128)(2,1)S(1)}, u32[]{:S(2)}, u32[]{:S(2)}) collective-permute-start(bf16[1,8,3,1024]{3,2,1,0:T(4,128)(2,1)S(1)} %get-tuple-element.112), channel_id=1, source_target_pairs={{0,1},{1,2},{2,3},{3,4},{4,5},{5,6},{6,7},{7,8},{8,9},{9,10},{10,1... | collective-permute-start | bytes 147464 | tf_op jit(solution)/shard_map/ppermute | solution.py:14
  45.9 392.1 %collective-permute-start.2 = (bf16[1,3,3,1024]{3,2,1,0:T(4,128)(2,1)S(1)}, bf16[1,3,3,1024]{3,2,1,0:T(4,128)(2,1)S(1)}, u32[]{:S(2)}, u32[]{:S(2)}) collective-permute-start(bf16[1,3,3,1024]{3,2,1,0:T(4,128)(2,1)S(1)} %get-tuple-element.109), channel_id=1, source_target_pairs={{0,3},{1,4},{2,5},{3,6},{4,7},{5,8},{6,9},{7,10},{8,11},{9,12},{10... | collective-permute-start | bytes 55304 | tf_op jit(solution)/shard_map/ppermute | solution.py:14
  47.9 287.7 %copy-start.125 = (bf16[6]{0:T(256)(128)(2,1)S(1)}, bf16[6]{0:T(256)(128)(2,1)}, u32[]{:S(2)}) copy-start(bf16[6]{0:T(256)(128)(2,1)} %param.15) | copy-start | bytes 40
  47.9 408.2 %collective-permute-start.1 = (bf16[1,3,16,1024]{3,2,1,0:T(8,128)(2,1)S(1)}, bf16[1,3,16,1024]{3,2,1,0:T(8,128)(2,1)S(1)}, u32[]{:S(2)}, u32[]{:S(2)}) collective-permute-start(bf16[1,3,16,1024]{3,2,1,0:T(8,128)(2,1)S(1)} %get-tuple-element.110), channel_id=1, source_target_pairs={{0,4},{1,5},{2,6},{3,7},{4,8},{5,9},{6,10},{7,11},{8,12},{9,13},{1... | collective-permute-start | bytes 294920 | tf_op jit(solution)/shard_map/ppermute | solution.py:14
  52.2 390.7 %collective-permute-start = (bf16[1,3,3,1024]{3,2,1,0:T(4,128)(2,1)S(1)}, bf16[1,3,3,1024]{3,2,1,0:T(4,128)(2,1)S(1)}, u32[]{:S(2)}, u32[]{:S(2)}) collective-permute-start(bf16[1,3,3,1024]{3,2,1,0:T(4,128)(2,1)S(1)} %get-tuple-element.106), channel_id=1, source_target_pairs={{0,5},{1,6},{2,7},{3,8},{4,9},{5,10},{6,11},{7,12},{8,13},{9,14},{... | collective-permute-start | bytes 55304 | tf_op jit(solution)/shard_map/ppermute | solution.py:14
  438.0 8.8 collective-permute-start.7
  443.0 13.2 collective-permute-start.6
  446.8 9.1 collective-permute-start.5
  1046.1 106.4 %collective-permute-start.12 = (bf16[1,3,3,1024]{3,2,1,0:T(4,128)(2,1)}, bf16[1,3,3,1024]{3,2,1,0:T(4,128)(2,1)S(1)}, u32[]{:S(2)}, u32[]{:S(2)}) collective-permute-start(bf16[1,3,3,1024]{3,2,1,0:T(4,128)(2,1)} %get-tuple-element.101), channel_id=1, source_target_pairs={{5,0},{6,1},{7,2},{8,3},{9,4},{10,5},{11,6},{12,7},{13,8},{14,9},{... | collective-permute-start | bytes 55304 | tf_op jit(solution)/shard_map/ppermute | solution.py:14
  1048.2 129.5 %collective-permute-start.11 = (bf16[1,3,16,1024]{3,2,1,0:T(8,128)(2,1)S(1)}, bf16[1,3,16,1024]{3,2,1,0:T(8,128)(2,1)S(1)}, u32[]{:S(2)}, u32[]{:S(2)}) collective-permute-start(bf16[1,3,16,1024]{3,2,1,0:T(8,128)(2,1)S(1)} %get-tuple-element.102), channel_id=1, source_target_pairs={{4,0},{5,1},{6,2},{7,3},{8,4},{9,5},{10,6},{11,7},{12,8},{13,9},{1... | collective-permute-start | bytes 294920 | tf_op jit(solution)/shard_map/ppermute | solution.py:14
  1055.5 98.9 %collective-permute-start.10 = (bf16[1,3,3,1024]{3,2,1,0:T(4,128)(2,1)}, bf16[1,3,3,1024]{3,2,1,0:T(4,128)(2,1)S(1)}, u32[]{:S(2)}, u32[]{:S(2)}) collective-permute-start(bf16[1,3,3,1024]{3,2,1,0:T(4,128)(2,1)} %get-tuple-element.98), channel_id=1, source_target_pairs={{3,0},{4,1},{5,2},{6,3},{7,4},{8,5},{9,6},{10,7},{11,8},{12,9},{13... | collective-permute-start | bytes 55304 | tf_op jit(solution)/shard_map/ppermute | solution.py:14
  1059.7 117.9 %collective-permute-start.9 = (bf16[1,8,3,1024]{3,2,1,0:T(4,128)(2,1)S(1)}, bf16[1,8,3,1024]{3,2,1,0:T(4,128)(2,1)S(1)}, u32[]{:S(2)}, u32[]{:S(2)}) collective-permute-start(bf16[1,8,3,1024]{3,2,1,0:T(4,128)(2,1)S(1)} %get-tuple-element.105), channel_id=1, source_target_pairs={{1,0},{2,1},{3,2},{4,3},{5,4},{6,5},{7,6},{8,7},{9,8},{10,9},{11,1... | collective-permute-start | bytes 147464 | tf_op jit(solution)/shard_map/ppermute | solution.py:14
  1061.6 116.0 %collective-permute-start.8 = (bf16[1,8,3,1024]{3,2,1,0:T(4,128)(2,1)S(1)}, bf16[1,8,3,1024]{3,2,1,0:T(4,128)(2,1)S(1)}, u32[]{:S(2)}, u32[]{:S(2)}) collective-permute-start(bf16[1,8,3,1024]{3,2,1,0:T(4,128)(2,1)S(1)} %get-tuple-element.104), channel_id=1, source_target_pairs={{0,1},{1,2},{2,3},{3,4},{4,5},{5,6},{6,7},{7,8},{8,9},{9,10},{10,1... | collective-permute-start | bytes 147464 | tf_op jit(solution)/shard_map/ppermute | solution.py:14
  1152.5 12.1 collective-permute-start.15
  1154.5 23.3 %collective-permute-start.14 = (bf16[1,3,16,1024]{3,2,1,0:T(8,128)(2,1)S(1)}, bf16[1,3,16,1024]{3,2,1,0:T(8,128)(2,1)S(1)}, u32[]{:S(2)}, u32[]{:S(2)}) collective-permute-start(bf16[1,3,16,1024]{3,2,1,0:T(8,128)(2,1)S(1)} %get-tuple-element.103), channel_id=1, source_target_pairs={{0,4},{1,5},{2,6},{3,7},{4,8},{5,9},{6,10},{7,11},{8,12},{9,13},{1... | collective-permute-start | bytes 294920 | tf_op jit(solution)/shard_map/ppermute | solution.py:14
  1164.6 12.9 collective-permute-start.13
  (123 other events, 10558.4 us)
Sparse Core Ops, SparseCore 0:
  10.2 989.5 all-gather.3
  1067.6 91.1 reduce-scatter.3
